TPU v7x, 128 devices: a whole 4x4x4 slice. The times are simulated.
128 devices in a mesh: mod: 16 (over x, y_hi, core), sp: 8 (over y_lo, z).
Axes of the slice: x: 4, y: 4 (y_hi: 2, y_lo: 2; y = y_hi * 2 + y_lo), z: 4, core: 2. Of those that a mesh axis runs over, the one named last changes fastest.
Arguments:
- images: bfloat16 [16, 512, 64, 256], P('mod', None, 'sp'), may hold values from -6 to 6
- conv_first: bfloat16 [16, 256, 256], P('mod'), may hold values from -0.375 to 0.375
- conv_second: bfloat16 [16, 4096, 256], P('mod'), may hold values from -0.09375 to 0.09375
- project: bfloat16 [16, 256, 512], P('mod'), may hold values from -0.375 to 0.375
- whiten: bfloat16 [16, 512, 256], P('mod'), may hold values from -0.25 to 0.25
- valid_mask: int32 [16, 512, 16, 4], P('mod', None, 'sp'), may hold values 0 or 1
- scene_index: int32 [512], replicated, may hold values from 0 to 63
Outputs:
- target: float32 [512, 256], P('sp')
- grad_view: bfloat16 [16, 512, 256], P('mod', 'sp')
- grad_whiten: float32 [16, 512, 256], P('mod', 'sp')
Inputs may be any that keep to these rules, and one draw needn't show every extreme that they name: `valid_mask`: 1 where a pixel of the encoded map is cloud-free.
All inputs are finite; a program needn't handle non-finite values. No bound on the sum of `valid_mask` on one device may be relied on, other than what follows from the above.
Results may differ from a plain program's by a relative error of at most 0.028.
Values may be sent and summed in bfloat16 or wider, within the bound.
No kernel may reach another device: no remote copies, remote signals or barrier semaphores. Data moves between devices by JAX's collectives and lax.ppermute only.
A program may use at most 192 MiB of HBM per device.

v0:
```python
import jax
import jax.numpy as jnp
from jax import lax
from jax.sharding import PartitionSpec as P

BANDS = 16
CH = 256
SCENES = 64


def extended(x, sides, width):
    for axis, dim in sides:
        size, length = (lax.axis_size(axis), x.shape[dim])
        up = [(i, (i + 1) % size) for i in range(size - 1)]
        down = [(j, i) for i, j in up]
        last = lax.slice_in_dim(x, length - width, length, axis=dim)
        leading = lax.slice_in_dim(x, 0, width, axis=dim)
        before = lax.ppermute(last, axis, up)
        after = lax.ppermute(leading, axis, down)
        x = jnp.concatenate([before, x, after], axis=dim)
    return x


def stride_conv(padded, weight, depth, per_tap):
    count, rows_in, wide = padded.shape
    columns = wide // depth
    sided = jnp.pad(padded, ((0, 0), (0, 0), (depth, depth)))
    paired = sided.reshape(count, rows_in, columns // 2 + 1, 2 * depth)
    joined = jnp.concatenate([paired[:, :, :-1], paired[:, :, 1:]], axis=-1)
    rows_out = (rows_in - 2) // 2
    span = 4 * depth
    taps = [joined[:, offset : offset + 2 * rows_out : 2] for offset in range(4)]
    if per_tap:
        total = jnp.zeros((count * rows_out * (columns // 2), weight.shape[1]), jnp.float32)
        for offset in range(4):
            total = total + jnp.dot(
                taps[offset].reshape(-1, span),
                weight[offset * span : (offset + 1) * span],
                preferred_element_type=jnp.float32,
            )
    else:
        total = jnp.dot(
            jnp.concatenate(taps, axis=-1).reshape(-1, 4 * span),
            weight,
            preferred_element_type=jnp.float32,
        )
    return (
        jnp.maximum(total, 0.0)
        .astype(jnp.bfloat16)
        .reshape(count, rows_out, columns // 2 * weight.shape[1])
    )


def make_view(feat, onehot_rows, scene_sums, counts, whiten_w):
    means = scene_sums / jnp.maximum(counts, 1.0)[:, None]
    panel = (feat - jnp.dot(onehot_rows, means, precision=lax.Precision.HIGHEST)).astype(
        jnp.bfloat16
    )
    raw = jnp.dot(panel, whiten_w, preferred_element_type=jnp.float32)
    scale = 1.0 / jnp.sqrt(jnp.mean(raw * raw, axis=-1, keepdims=True) + 1e-05)
    return (panel, scale, (raw * scale).astype(jnp.bfloat16))


def on_device(images, conv_first, conv_second, project, whiten, valid_mask, scene_index):
    samples = images.shape[1]
    share = samples // lax.axis_size("sp")
    first_row = lax.axis_index("sp") * share
    padded = extended(images[0], (("sp", 1),), 1)
    first = stride_conv(padded, conv_first[0], BANDS, False)
    widened = extended(first, (("sp", 1),), 1)
    second = stride_conv(widened, conv_second[0], CH, True)
    pixels = second.reshape(samples, -1, CH)
    mask_rows = valid_mask[0].reshape(samples, -1).astype(jnp.bfloat16)
    cells = pixels.shape[1] * lax.axis_size("sp")
    pooled_part = (
        jnp.einsum("npc,np->nc", pixels, mask_rows, preferred_element_type=jnp.float32) / cells
    )
    pooled_rows = lax.psum_scatter(pooled_part, "sp", scatter_dimension=0, tiled=True)
    onehot = (scene_index[:, None] == jnp.arange(SCENES, dtype=jnp.int32)[None, :]).astype(
        jnp.float32
    )
    counts = jnp.sum(onehot, axis=0)
    project_w = project[0]
    whiten_w = whiten[0]
    feat = jnp.dot(pooled_rows.astype(jnp.bfloat16), project_w, preferred_element_type=jnp.float32)
    onehot_rows = lax.dynamic_slice_in_dim(onehot, first_row, share, 0)
    local_sums = jnp.dot(onehot_rows.T, feat, precision=lax.Precision.HIGHEST)
    scene_sums = lax.psum(local_sums, "sp")
    panel_rows, scale_rows, view_rows = make_view(feat, onehot_rows, scene_sums, counts, whiten_w)
    view = lax.all_gather(view_rows, "sp", axis=0, tiled=True)
    width = view.shape[1]
    eye = jnp.eye(width, dtype=jnp.float32)
    total = lax.psum(view.astype(jnp.float32).astype(jnp.bfloat16), "mod").astype(jnp.float32)
    piece = lax.all_gather(view[None], "mod", axis=0, tiled=True)
    blocks = jnp.einsum("nk,pnl->pkl", view, piece, preferred_element_type=jnp.float32) / samples
    piece_rows = lax.dynamic_slice_in_dim(piece, first_row, share, 1).astype(jnp.float32)
    coupling = jnp.einsum("pnl,pkl->nk", piece_rows, blocks - eye, precision=lax.Precision.HIGHEST)
    mean_view = total / lax.axis_size("mod")
    gram = jnp.dot(mean_view.T, mean_view, precision=lax.Precision.HIGHEST) / samples + 0.001 * eye
    lower = jnp.linalg.cholesky(gram)
    mean_rows = lax.dynamic_slice_in_dim(mean_view, first_row, share, 0)
    target_rows = jax.scipy.linalg.solve_triangular(lower, mean_rows.T, lower=True).T
    view_f = view_rows.astype(jnp.float32)
    grad_full = view_f - target_rows + coupling
    inner = jnp.mean(grad_full * view_f, axis=-1, keepdims=True)
    grad_raw = ((grad_full - view_f * inner) * scale_rows).astype(jnp.bfloat16)
    grad_w = lax.psum_scatter(
        jnp.dot(panel_rows.T, grad_raw, preferred_element_type=jnp.float32).astype(jnp.bfloat16),
        "sp",
        scatter_dimension=0,
        tiled=True,
    ).astype(jnp.float32)
    return (target_rows, grad_full.astype(jnp.bfloat16)[None], grad_w[None])


def solution(mesh):
    placed = (
        P("mod", None, "sp", None),
        P("mod", None, None),
        P("mod", None, None),
        P("mod", None, None),
        P("mod", None, None),
        P("mod", None, "sp", None),
        P(),
    )
    return jax.shard_map(
        on_device,
        mesh=mesh,
        in_specs=placed,
        out_specs=(P("sp", None), P("mod", "sp", None), P("mod", "sp", None)),
        check_vma=False,
    )
```

profile of v0, /device:TPU:0, one launch (start us, length us, event | category | flops | bytes accessed | tf_op | source)
XLA Modules:
  0.0 805.1 jit_solution(15705632569282844667)
XLA Ops:
  7.2 3.0 copy.29
  10.3 3.9 collective-permute-start
  14.3 1.3 collective-permute-start.1
  15.6 4.2 collective-permute-done
  19.8 4.3 collective-permute-done.1
  26.7 3.6 pad_maximum_fusion.1
  30.3 14.7 %copy.30 = bf16[512,4,8,256]{3,2,1,0:T(8,128)(2,1)} copy(bf16[512,4,8,256]{0,3,2,1:T(8,128)(2,1)} %pad_maximum_fusion.1) | data formatting | bytes 16777216 | tf_op jit(solution)/shard_map/concatenate | solution.py:43
  45.0 9.0 %fusion.1 = bf16[16384,256]{1,0:T(8,128)(2,1)} fusion(bf16[16384,256]{1,0:T(8,128)(2,1)} %bitcast.98, bf16[1,256,256]{2,1,0:T(8,128)(2,1)S(1)} %copy-done.4), kind=kOutput, calls=%fused_computation.7 | convolution fusion | flops 2155872256 | bytes 16908288 | tf_op jit(solution)/shard_map/dot_general | solution.py:42
  54.0 14.6 %reshape.81 = bf16[512,4,2048]{2,1,0:T(4,128)(2,1)} reshape(bf16[16384,256]{1,0:T(8,128)(2,1)} %fusion.1) | data formatting | bytes 16777216 | tf_op jit(solution)/shard_map/reshape | solution.py:50
  68.5 13.7 %copy.31 = bf16[512,4,2048]{0,2,1:T(8,128)(2,1)} copy(bf16[512,4,2048]{2,1,0:T(4,128)(2,1)} %reshape.81) | data formatting | bytes 16777216 | tf_op jit(solution)/shard_map/reshape | solution.py:50
  82.2 4.6 fusion.73
  86.8 3.8 collective-permute-start.2
  90.5 1.3 collective-permute-start.3
  92.1 42.4 %collective-permute-done.2 = bf16[512,1,2048]{0,2,1:T(8,128)(2,1)S(1)} collective-permute-done((bf16[512,1,2048]{0,2,1:T(8,128)(2,1)}, bf16[512,1,2048]{0,2,1:T(8,128)(2,1)S(1)}, u32[]{:S(2)}, u32[]{:S(2)}) %collective-permute-start.2) | collective-permute-done | bytes 2097184 | tf_op jit(solution)/shard_map/ppermute | solution.py:18
  134.5 4.2 collective-permute-done.3
  138.7 11.7 %fusion.6 = bf16[512,6,2560]{0,2,1:T(8,128)(2,1)S(1)} fusion(bf16[512,1,2048]{0,2,1:T(8,128)(2,1)} %collective-permute-done.3, bf16[512,4,2048]{0,2,1:T(8,128)(2,1)} %copy.31, bf16[512,1,2048]{0,2,1:T(8,128)(2,1)S(1)} %collective-permute-done.2), kind=kLoop, calls=%fused_computation.12 | loop fusion | flops 94371840 | bytes 28311552 | tf_op jit(solution)/shard_map/concatenate | solution.py:20
  150.4 8.6 %fusion.72 = (bf16[512,6,4,512]{0,3,2,1:T(8,128)(2,1)}, bf16[512,6,4,512]{0,3,2,1:T(8,128)(2,1)}) fusion(bf16[512,6,5,512]{0,3,2,1:T(8,128)(2,1)S(1)} %bitcast.97), kind=kLoop, calls=%fused_computation.121 | loop fusion | bytes 50331648 | tf_op jit(solution)/shard_map/slice | solution.py:29
  159.0 20.2 %pad_maximum_fusion = bf16[512,6,4,1024]{0,3,2,1:T(8,128)(2,1)} fusion(bf16[512,6,4,512]{0,3,2,1:T(8,128)(2,1)} %get-tuple-element.26, bf16[512,6,4,512]{0,3,2,1:T(8,128)(2,1)} %get-tuple-element.25), kind=kLoop, calls=%fused_computation.5 | loop fusion | flops 50331648 | bytes 50331648 | tf_op jit(solution)/shard_map/concatenate | solution.py:29
  179.2 22.9 %fusion.71 = (bf16[512,2,4,1024]{0,3,2,1:T(8,128)(2,1)}, bf16[512,2,4,1024]{0,3,2,1:T(8,128)(2,1)}, bf16[512,2,4,1024]{0,3,2,1:T(8,128)(2,1)}, bf16[512,2,4,1024]{0,3,2,1:T(8,128)(2,1)}) fusion(bf16[512,6,4,1024]{0,3,2,1:T(8,128)(2,1)} %pad_maximum_fusion), kind=kLoop, calls=%fused_computation.120 | loop fusion | bytes 67108864 | tf_op jit(solution)/shard_map/slice | solution.py:32
  202.1 14.9 %copy.34 = bf16[512,2,4,1024]{3,2,1,0:T(4,128)(2,1)} copy(bf16[512,2,4,1024]{0,3,2,1:T(8,128)(2,1)} %get-tuple-element.24) | data formatting | bytes 16777216 | tf_op jit(solution)/shard_map/slice | solution.py:32
  217.0 12.6 %reshape.83 = bf16[4096,1024]{1,0:T(8,128)(2,1)} reshape(bf16[512,2,4,1024]{3,2,1,0:T(4,128)(2,1)} %copy.34) | data formatting | bytes 16777216 | tf_op jit(solution)/shard_map/reshape | solution.py:37
  229.5 14.9 %copy.35 = bf16[512,2,4,1024]{3,2,1,0:T(4,128)(2,1)} copy(bf16[512,2,4,1024]{0,3,2,1:T(8,128)(2,1)} %get-tuple-element.23) | data formatting | bytes 16777216 | tf_op jit(solution)/shard_map/slice | solution.py:32
  244.4 12.5 %reshape.84 = bf16[4096,1024]{1,0:T(8,128)(2,1)} reshape(bf16[512,2,4,1024]{3,2,1,0:T(4,128)(2,1)} %copy.35) | data formatting | bytes 16777216 | tf_op jit(solution)/shard_map/reshape | solution.py:37
  256.9 14.9 %copy.36 = bf16[512,2,4,1024]{3,2,1,0:T(4,128)(2,1)} copy(bf16[512,2,4,1024]{0,3,2,1:T(8,128)(2,1)} %get-tuple-element.22) | data formatting | bytes 16777216 | tf_op jit(solution)/shard_map/slice | solution.py:32
  271.8 12.6 %reshape.85 = bf16[4096,1024]{1,0:T(8,128)(2,1)} reshape(bf16[512,2,4,1024]{3,2,1,0:T(4,128)(2,1)} %copy.36) | data formatting | bytes 16777216 | tf_op jit(solution)/shard_map/reshape | solution.py:37
  284.4 14.9 %copy.37 = bf16[512,2,4,1024]{3,2,1,0:T(4,128)(2,1)} copy(bf16[512,2,4,1024]{0,3,2,1:T(8,128)(2,1)} %get-tuple-element.21) | data formatting | bytes 16777216 | tf_op jit(solution)/shard_map/slice | solution.py:32
  299.3 13.1 %reshape.86 = bf16[4096,1024]{1,0:T(8,128)(2,1)} reshape(bf16[512,2,4,1024]{3,2,1,0:T(4,128)(2,1)} %copy.37) | data formatting | bytes 16777216 | tf_op jit(solution)/shard_map/reshape | solution.py:37
  312.4 6.0 fusion.28
  318.4 6.0 convolution_add_fusion.2
  324.4 4.6 convolution_add_fusion.1
  329.0 7.6 fusion.17
  337.7 41.9 %reduce-scatter.3.cloned.1.call-done = f32[64,256]{1,0:T(8,128)} async-done(((f32[512,256]{1,0:T(8,128)}), f32[64,256]{1,0:T(8,128)}) %reduce-scatter.3.cloned.1.call-update) | async-done | bytes 65552 | tf_op jit(solution)/shard_map/reduce_scatter | solution.py:78
  381.6 73.5 %all-reduce.6.cloned.1.call-done = f32[64,512]{1,0:T(8,128)} async-done(((f32[64,512]{1,0:T(8,128)}), f32[64,512]{1,0:T(8,128)}) %all-reduce.6.cloned.1.call-update) | async-done | bytes 131088 | tf_op jit(solution)/shard_map/psum | solution.py:88
  456.6 30.5 %all_gather.6 = bf16[512,256]{1,0:T(8,128)(2,1)} all-gather(bf16[64,256]{1,0:T(8,128)(2,1)S(1)} %multiply_convert_fusion), channel_id=1, replica_groups=mesh['mod'=16,'sp'=8] {'sp'}, dimensions={0}, use_global_device_ids=true | all-gather | bytes 294912 | tf_op jit(solution)/shard_map/all_gather | solution.py:90
  487.2 54.9 %all-gather.3.cloned.1.call-done = bf16[8192,256]{1,0:T(8,128)(2,1)} async-done(((bf16[512,256]{1,0:T(8,128)(2,1)}), bf16[8192,256]{1,0:T(8,128)(2,1)}) %all-gather.3.cloned.1.call-update) | async-done | bytes 4194320 | tf_op jit(solution)/shard_map/all_gather | solution.py:94
  542.1 5.5 fusion.36
  548.5 139.4 %all-reduce.8.cloned.1.call-done = bf16[512,256]{1,0:T(8,128)(2,1)} async-done(((bf16[512,256]{1,0:T(8,128)(2,1)}), bf16[512,256]{1,0:T(8,128)(2,1)}) %all-reduce.8.cloned.1.call-update) | async-done | bytes 262160 | tf_op jit(solution)/shard_map/psum | solution.py:93
  687.9 2.0 convolution_multiply_fusion
  690.2 11.7 %cholesky.49 = f32[128,128]{1,0:T(8,128)S(1)} custom-call(f32[128,128]{1,0:T(8,128)S(1)} %cholesky.115), custom_call_target="Cholesky" | custom-call | tf_op jit(solution)/shard_map/jit(cholesky)/cholesky | solution.py:100
  702.0 9.8 %custom-call.15 = f32[1,128,128]{1,2,0:T(8,128)S(1)} custom-call(f32[1,128,128]{2,1,0:T(8,128)S(1)} %get-tuple-element.42), custom_call_target="InvertDiagBlocksLowerTriangular" | custom-call | tf_op jit(solution)/shard_map/jit(cholesky)/cholesky | solution.py:100
  712.3 11.7 %cholesky.103 = f32[128,128]{1,0:T(8,128)S(1)} custom-call(f32[128,128]{1,0:T(8,128)S(1)} %convolution_subtract_fusion.1), custom_call_target="Cholesky" | custom-call | tf_op jit(solution)/shard_map/jit(cholesky)/cholesky | solution.py:100
  726.1 4.2 while.1
  726.9 1.4 bitcast_dynamic-update-slice_fusion.2
  728.9 1.4 bitcast_dynamic-update-slice_fusion.2
  730.3 19.7 %custom-call.16 = f32[2,128,128]{1,2,0:T(8,128)S(1)} custom-call(f32[2,128,128]{2,1,0:T(8,128)S(1)} %get-tuple-element.10), custom_call_target="InvertDiagBlocksLowerTriangular" | custom-call | tf_op jit(solution)/shard_map/jit(_solve_triangular)/triangular_solve | solution.py:102
  751.6 4.3 fusion.23
  757.7 39.3 %reduce-scatter.5.cloned.1.call-done = bf16[64,256]{1,0:T(8,128)(2,1)} async-done(((bf16[512,256]{1,0:T(8,128)(2,1)}), bf16[64,256]{1,0:T(8,128)(2,1)}) %reduce-scatter.5.cloned.1.call-update) | async-done | bytes 32784 | tf_op jit(solution)/shard_map/reduce_scatter | solution.py:107
  797.0 1.4 bitcast_convert_fusion
  (75 shorter events, 14.4 us)
Async XLA Ops:
  7.2 372.4 %copy-start = (bf16[1,256,512]{2,1,0:T(8,128)(2,1)S(1)}, bf16[1,256,512]{2,1,0:T(8,128)(2,1)}, u32[]{:S(2)}) copy-start(bf16[1,256,512]{2,1,0:T(8,128)(2,1)} %param.10) | copy-start | bytes 786436
  7.2 372.4 %reduce-scatter.3.cloned.1.call-start = ((), (), s32[]{:S(2)}) async-start(), calls=%async_computation.2 | async-start | bytes 589824 | tf_op jit(solution)/shard_map/reduce_scatter | solution.py:78
  10.3 9.5 %collective-permute-start = (bf16[512,1,256]{0,2,1:T(8,128)(2,1)S(1)}, bf16[512,1,256]{0,2,1:T(8,128)(2,1)S(1)}, u32[]{:S(2)}, u32[]{:S(2)}) collective-permute-start(bf16[512,1,256]{0,2,1:T(8,128)(2,1)S(1)} %get-tuple-element.35), channel_id=1, source_target_pairs={{0,1},{1,2},{2,3},{3,4},{4,5},{5,6},{6,7},{8,9},{9,10},{10,11},{11... | collective-permute-start | bytes 786440 | tf_op jit(solution)/shard_map/ppermute | solution.py:18
  14.3 9.8 %collective-permute-start.1 = (bf16[512,1,256]{0,2,1:T(8,128)(2,1)S(1)}, bf16[512,1,256]{0,2,1:T(8,128)(2,1)S(1)}, u32[]{:S(2)}, u32[]{:S(2)}) collective-permute-start(bf16[512,1,256]{0,2,1:T(8,128)(2,1)S(1)} %get-tuple-element.36), channel_id=1, source_target_pairs={{1,0},{2,1},{3,2},{4,3},{5,4},{6,5},{7,6},{9,8},{10,9},{11,10},{12... | collective-permute-start | bytes 786440 | tf_op jit(solution)/shard_map/ppermute | solution.py:19
  30.3 14.7 %copy-start.4 = (bf16[1,256,256]{2,1,0:T(8,128)(2,1)S(1)}, bf16[1,256,256]{2,1,0:T(8,128)(2,1)}, u32[]{:S(2)}) copy-start(bf16[1,256,256]{2,1,0:T(8,128)(2,1)} %param.8) | copy-start | bytes 393220
  82.2 9.6 %copy-start.5 = (s32[1,512,2,4]{1,3,2,0:T(4,128)S(1)}, s32[1,512,2,4]{1,3,2,0:T(4,128)}, u32[]{:S(2)}) copy-start(s32[1,512,2,4]{1,3,2,0:T(4,128)} %param.12) | copy-start | bytes 49156
  86.8 47.7 %collective-permute-start.2 = (bf16[512,1,2048]{0,2,1:T(8,128)(2,1)}, bf16[512,1,2048]{0,2,1:T(8,128)(2,1)S(1)}, u32[]{:S(2)}, u32[]{:S(2)}) collective-permute-start(bf16[512,1,2048]{0,2,1:T(8,128)(2,1)} %get-tuple-element.27), channel_id=1, source_target_pairs={{0,1},{1,2},{2,3},{3,4},{4,5},{5,6},{6,7},{8,9},{9,10},{10,11},{11... | collective-permute-start | bytes 6291464 | tf_op jit(solution)/shard_map/ppermute | solution.py:18
  90.5 48.2 %collective-permute-start.3 = (bf16[512,1,2048]{0,2,1:T(8,128)(2,1)}, bf16[512,1,2048]{0,2,1:T(8,128)(2,1)}, u32[]{:S(2)}, u32[]{:S(2)}) collective-permute-start(bf16[512,1,2048]{0,2,1:T(8,128)(2,1)} %get-tuple-element.28), channel_id=1, source_target_pairs={{1,0},{2,1},{3,2},{4,3},{5,4},{6,5},{7,6},{9,8},{10,9},{11,10},{12... | collective-permute-start | bytes 6291464 | tf_op jit(solution)/shard_map/ppermute | solution.py:19
  299.3 13.1 %copy-start.1 = (bf16[1,4096,256]{2,1,0:T(8,128)(2,1)S(1)}, bf16[1,4096,256]{2,1,0:T(8,128)(2,1)}, u32[]{:S(2)}) copy-start(bf16[1,4096,256]{2,1,0:T(8,128)(2,1)} %param.9) | copy-start | bytes 6291460
  312.4 12.0 %slice-start = ((s8[8388608]{0:T(1024)(128)(4,1)}), s8[4194304]{0:T(1024)(128)(4,1)S(1)}, s32[]{:S(2)}) async-start(s8[8388608]{0:T(1024)(128)(4,1)} %bitcast.99), calls=%async_computation.7 | async-start | bytes 8388608
  318.4 6.0 slice-start.1
  329.0 8.6 %copy-start.6 = (s32[512]{0:T(512)S(1)}, s32[512]{0:T(512)}, u32[]{:S(2)}) copy-start(s32[512]{0:T(512)} %param.13) | copy-start | bytes 6148
  329.0 127.3 %copy-start.3 = (bf16[1,512,256]{2,1,0:T(8,128)(2,1)S(1)}, bf16[1,512,256]{2,1,0:T(8,128)(2,1)}, u32[]{:S(2)}) copy-start(bf16[1,512,256]{2,1,0:T(8,128)(2,1)} %param.11) | copy-start | bytes 786436
  337.5 117.5 %all-reduce.6.cloned.1.call-start = ((), (), s32[]{:S(2)}) async-start(), calls=%async_computation.3 | async-start | bytes 262144 | tf_op jit(solution)/shard_map/psum | solution.py:88
  381.5 160.6 %all-gather.3.cloned.1.call-start = ((), (), s32[]{:S(2)}) async-start(), calls=%async_computation.6 | async-start | bytes 4456448 | tf_op jit(solution)/shard_map/all_gather | solution.py:94
  547.6 140.4 %all-reduce.8.cloned.1.call-start = ((), (), s32[]{:S(2)}) async-start(), calls=%async_computation.4 | async-start | bytes 524288 | tf_op jit(solution)/shard_map/psum | solution.py:93
  548.1 248.9 %reduce-scatter.5.cloned.1.call-start = ((), (), s32[]{:S(2)}) async-start(), calls=%async_computation.5 | async-start | bytes 294912 | tf_op jit(solution)/shard_map/reduce_scatter | solution.py:107
  751.6 46.8 %copy-start.2 = (f32[64,256]{1,0:T(8,128)}, f32[64,256]{1,0:T(8,128)S(1)}, u32[]{:S(2)}) copy-start(f32[64,256]{1,0:T(8,128)S(1)} %maximum_bitcast_fusion) | copy-start | bytes 196612
Sparse Core Ops, SparseCore 0:
  337.6 41.8 reduce-scatter.2
  382.0 72.9 all-reduce.5
  487.3 54.7 all-gather.2
  550.5 137.3 all-reduce.7
  757.8 39.1 reduce-scatter.4
where the time goes:
time: 817 us; the launch traced here: 805 us
  waiting for transfers between devices  405 us (50%)
  local copies, waits for them, and re-layouts  199 us (24%)
  other arithmetic  94.3 us (12%)
  matrix products  50.4 us (6%)
  blocking collectives  30.5 us (4%)
  between operations  15.7 us (2%)
  starting transfers between devices  10.6 us (1%)
    psum x1, waiting for transfers between devices, on_device(): lax.psum(view.astype(jnp.float32).astype(jnp.bfloat16), 'mod')  139 us
    slice x6, local copies, waits for them, and re-layouts, stride_conv(): taps = [joined[:, offset:offset + 2 * rows_out:2] for offset in range(4)]  83.5 us
    psum x1, waiting for transfers between devices, on_device(): scene_sums = lax.psum(local_sums, 'sp')  73.5 us
    all_gather x1, waiting for transfers between devices, on_device(): piece = lax.all_gather(view[None], 'mod', axis=0, tiled=True)  54.9 us
    reshape x4, local copies, waits for them, and re-layouts, stride_conv(): taps[offset].reshape(-1, span)  50.7 us
    ppermute x2, waiting for transfers between devices, extended(): before = lax.ppermute(last, axis, up)  46.6 us
    reduce_scatter x1, waiting for transfers between devices, on_device(): lax.psum_scatter(pooled_part, 'sp', scatter_dimension=0, tiled=True)  41.9 us
    reduce_scatter x1, waiting for transfers between devices, on_device(): lax.psum_scatter(jnp.dot(panel_rows.T, grad_raw, preferred_element_type=j...  39.3 us
  transfers between devices with their start and end apart: 9, of which 9 were waited for; matrix products, arithmetic and copies ran while one was open for 0% of the time, Pallas kernels for 0%

commit v1 on v0

--- a/solution.py
+++ b/solution.py
@@ -85,7 +85,7 @@
     feat = jnp.dot(pooled_rows.astype(jnp.bfloat16), project_w, preferred_element_type=jnp.float32)
     onehot_rows = lax.dynamic_slice_in_dim(onehot, first_row, share, 0)
     local_sums = jnp.dot(onehot_rows.T, feat, precision=lax.Precision.HIGHEST)
-    scene_sums = lax.psum(local_sums, "sp")
+    scene_sums = jnp.sum(lax.all_gather(local_sums, "sp"), axis=0)
     panel_rows, scale_rows, view_rows = make_view(feat, onehot_rows, scene_sums, counts, whiten_w)
     view = lax.all_gather(view_rows, "sp", axis=0, tiled=True)
     width = view.shape[1]

time: 817 us -> 782 us (0.957)
  waiting for transfers between devices: 405 us -> 369 us
    psum x1 -> x0, waiting for transfers between devices: 73.5 us -> none  [on_device(): scene_sums = lax.psum(local_sums, 'sp')]
    all_gather x0 -> x1, waiting for transfers between devices: none -> 37.7 us  [on_device(): scene_sums = jnp.sum(lax.all_gather(local_sums, 'sp'), axis=0)]
where the time goes in v1:
time: 782 us; the launch traced here: 770 us
  waiting for transfers between devices  369 us (47%)
  local copies, waits for them, and re-layouts  199 us (25%)
  other arithmetic  95.6 us (12%)
  matrix products  49.5 us (6%)
  blocking collectives  30.6 us (4%)
  between operations  15.7 us (2%)
  starting transfers between devices  10.6 us (1%)
    psum x1, waiting for transfers between devices, on_device(): lax.psum(view.astype(jnp.float32).astype(jnp.bfloat16), 'mod')  140 us
    slice x6, local copies, waits for them, and re-layouts, stride_conv(): taps = [joined[:, offset:offset + 2 * rows_out:2] for offset in range(4)]  83.5 us
    all_gather x1, waiting for transfers between devices, on_device(): piece = lax.all_gather(view[None], 'mod', axis=0, tiled=True)  54.9 us
    reshape x4, local copies, waits for them, and re-layouts, stride_conv(): taps[offset].reshape(-1, span)  50.7 us
    ppermute x2, waiting for transfers between devices, extended(): before = lax.ppermute(last, axis, up)  46.6 us
    reduce_scatter x1, waiting for transfers between devices, on_device(): lax.psum_scatter(pooled_part, 'sp', scatter_dimension=0, tiled=True)  42 us
    reduce_scatter x1, waiting for transfers between devices, on_device(): lax.psum_scatter(jnp.dot(panel_rows.T, grad_raw, preferred_element_type=j...  39.3 us
    all_gather x1, waiting for transfers between devices, on_device(): scene_sums = jnp.sum(lax.all_gather(local_sums, 'sp'), axis=0)  37.7 us
  transfers between devices with their start and end apart: 9, of which 9 were waited for; matrix products, arithmetic and copies ran while one was open for 0% of the time, Pallas kernels for 0%

profile of v1, /device:TPU:0, one launch (start us, length us, event | category | flops | bytes accessed | tf_op | source)
XLA Modules:
  0.0 770.2 jit_solution(16180472594324560484)
XLA Ops:
  7.2 3.0 copy.29
  10.3 3.9 collective-permute-start
  15.6 4.2 collective-permute-done
  19.8 4.3 collective-permute-done.1
  26.7 3.6 pad_maximum_fusion.1
  30.3 14.7 %copy.30 = bf16[512,4,8,256]{3,2,1,0:T(8,128)(2,1)} copy(bf16[512,4,8,256]{0,3,2,1:T(8,128)(2,1)} %pad_maximum_fusion.1) | data formatting | bytes 16777216 | tf_op jit(solution)/shard_map/concatenate | solution.py:43
  45.0 9.0 %fusion.1 = bf16[16384,256]{1,0:T(8,128)(2,1)} fusion(bf16[16384,256]{1,0:T(8,128)(2,1)} %bitcast.99, bf16[1,256,256]{2,1,0:T(8,128)(2,1)S(1)} %copy-done.4), kind=kOutput, calls=%fused_computation.7 | convolution fusion | flops 2155872256 | bytes 16908288 | tf_op jit(solution)/shard_map/dot_general | solution.py:42
  54.0 14.6 %reshape.81 = bf16[512,4,2048]{2,1,0:T(4,128)(2,1)} reshape(bf16[16384,256]{1,0:T(8,128)(2,1)} %fusion.1) | data formatting | bytes 16777216 | tf_op jit(solution)/shard_map/reshape | solution.py:50
  68.5 13.7 %copy.31 = bf16[512,4,2048]{0,2,1:T(8,128)(2,1)} copy(bf16[512,4,2048]{2,1,0:T(4,128)(2,1)} %reshape.81) | data formatting | bytes 16777216 | tf_op jit(solution)/shard_map/reshape | solution.py:50
  82.2 4.6 fusion.73
  86.8 3.8 collective-permute-start.2
  90.5 1.3 collective-permute-start.3
  92.1 42.4 %collective-permute-done.2 = bf16[512,1,2048]{0,2,1:T(8,128)(2,1)S(1)} collective-permute-done((bf16[512,1,2048]{0,2,1:T(8,128)(2,1)}, bf16[512,1,2048]{0,2,1:T(8,128)(2,1)S(1)}, u32[]{:S(2)}, u32[]{:S(2)}) %collective-permute-start.2) | collective-permute-done | bytes 2097184 | tf_op jit(solution)/shard_map/ppermute | solution.py:18
  134.5 4.2 collective-permute-done.3
  138.7 11.7 %fusion.6 = bf16[512,6,2560]{0,2,1:T(8,128)(2,1)S(1)} fusion(bf16[512,1,2048]{0,2,1:T(8,128)(2,1)} %collective-permute-done.3, bf16[512,4,2048]{0,2,1:T(8,128)(2,1)} %copy.31, bf16[512,1,2048]{0,2,1:T(8,128)(2,1)S(1)} %collective-permute-done.2), kind=kLoop, calls=%fused_computation.12 | loop fusion | flops 94371840 | bytes 28311552 | tf_op jit(solution)/shard_map/concatenate | solution.py:20
  150.4 8.6 %fusion.72 = (bf16[512,6,4,512]{0,3,2,1:T(8,128)(2,1)}, bf16[512,6,4,512]{0,3,2,1:T(8,128)(2,1)}) fusion(bf16[512,6,5,512]{0,3,2,1:T(8,128)(2,1)S(1)} %bitcast.98), kind=kLoop, calls=%fused_computation.121 | loop fusion | bytes 50331648 | tf_op jit(solution)/shard_map/slice | solution.py:29
  159.0 20.2 %pad_maximum_fusion = bf16[512,6,4,1024]{0,3,2,1:T(8,128)(2,1)} fusion(bf16[512,6,4,512]{0,3,2,1:T(8,128)(2,1)} %get-tuple-element.26, bf16[512,6,4,512]{0,3,2,1:T(8,128)(2,1)} %get-tuple-element.25), kind=kLoop, calls=%fused_computation.5 | loop fusion | flops 50331648 | bytes 50331648 | tf_op jit(solution)/shard_map/concatenate | solution.py:29
  179.2 22.9 %fusion.71 = (bf16[512,2,4,1024]{0,3,2,1:T(8,128)(2,1)}, bf16[512,2,4,1024]{0,3,2,1:T(8,128)(2,1)}, bf16[512,2,4,1024]{0,3,2,1:T(8,128)(2,1)}, bf16[512,2,4,1024]{0,3,2,1:T(8,128)(2,1)}) fusion(bf16[512,6,4,1024]{0,3,2,1:T(8,128)(2,1)} %pad_maximum_fusion), kind=kLoop, calls=%fused_computation.120 | loop fusion | bytes 67108864 | tf_op jit(solution)/shard_map/slice | solution.py:32
  202.1 14.9 %copy.34 = bf16[512,2,4,1024]{3,2,1,0:T(4,128)(2,1)} copy(bf16[512,2,4,1024]{0,3,2,1:T(8,128)(2,1)} %get-tuple-element.24) | data formatting | bytes 16777216 | tf_op jit(solution)/shard_map/slice | solution.py:32
  217.0 12.6 %reshape.83 = bf16[4096,1024]{1,0:T(8,128)(2,1)} reshape(bf16[512,2,4,1024]{3,2,1,0:T(4,128)(2,1)} %copy.34) | data formatting | bytes 16777216 | tf_op jit(solution)/shard_map/reshape | solution.py:37
  229.5 14.9 %copy.35 = bf16[512,2,4,1024]{3,2,1,0:T(4,128)(2,1)} copy(bf16[512,2,4,1024]{0,3,2,1:T(8,128)(2,1)} %get-tuple-element.23) | data formatting | bytes 16777216 | tf_op jit(solution)/shard_map/slice | solution.py:32
  244.4 12.5 %reshape.84 = bf16[4096,1024]{1,0:T(8,128)(2,1)} reshape(bf16[512,2,4,1024]{3,2,1,0:T(4,128)(2,1)} %copy.35) | data formatting | bytes 16777216 | tf_op jit(solution)/shard_map/reshape | solution.py:37
  256.9 14.9 %copy.36 = bf16[512,2,4,1024]{3,2,1,0:T(4,128)(2,1)} copy(bf16[512,2,4,1024]{0,3,2,1:T(8,128)(2,1)} %get-tuple-element.22) | data formatting | bytes 16777216 | tf_op jit(solution)/shard_map/slice | solution.py:32
  271.8 12.6 %reshape.85 = bf16[4096,1024]{1,0:T(8,128)(2,1)} reshape(bf16[512,2,4,1024]{3,2,1,0:T(4,128)(2,1)} %copy.36) | data formatting | bytes 16777216 | tf_op jit(solution)/shard_map/reshape | solution.py:37
  284.4 14.9 %copy.37 = bf16[512,2,4,1024]{3,2,1,0:T(4,128)(2,1)} copy(bf16[512,2,4,1024]{0,3,2,1:T(8,128)(2,1)} %get-tuple-element.21) | data formatting | bytes 16777216 | tf_op jit(solution)/shard_map/slice | solution.py:32
  299.3 13.1 %reshape.86 = bf16[4096,1024]{1,0:T(8,128)(2,1)} reshape(bf16[512,2,4,1024]{3,2,1,0:T(4,128)(2,1)} %copy.37) | data formatting | bytes 16777216 | tf_op jit(solution)/shard_map/reshape | solution.py:37
  312.4 6.0 fusion.28
  318.4 6.0 convolution_add_fusion.2
  324.4 4.6 convolution_add_fusion.1
  329.0 7.6 fusion.17
  337.6 42.0 %reduce-scatter.3.cloned.1.call-done = f32[64,256]{1,0:T(8,128)} async-done(((f32[512,256]{1,0:T(8,128)}), f32[64,256]{1,0:T(8,128)}) %reduce-scatter.3.cloned.1.call-update) | async-done | bytes 65552 | tf_op jit(solution)/shard_map/reduce_scatter | solution.py:78
  381.7 37.7 %all-gather.5.cloned.1.call-done = f32[512,512]{1,0:T(8,128)} async-done(((f32[64,512]{1,0:T(8,128)}), f32[512,512]{1,0:T(8,128)}) %all-gather.5.cloned.1.call-update) | async-done | bytes 1048592 | tf_op jit(solution)/shard_map/all_gather | solution.py:88
  419.4 1.3 reduce_sum.36
  421.4 30.6 %all_gather.14 = bf16[512,256]{1,0:T(8,128)(2,1)} all-gather(bf16[64,256]{1,0:T(8,128)(2,1)S(1)} %multiply_convert_fusion), channel_id=1, replica_groups=mesh['mod'=16,'sp'=8] {'sp'}, dimensions={0}, use_global_device_ids=true | all-gather | bytes 294912 | tf_op jit(solution)/shard_map/all_gather | solution.py:90
  452.0 54.9 %all-gather.7.cloned.1.call-done = bf16[8192,256]{1,0:T(8,128)(2,1)} async-done(((bf16[512,256]{1,0:T(8,128)(2,1)}), bf16[8192,256]{1,0:T(8,128)(2,1)}) %all-gather.7.cloned.1.call-update) | async-done | bytes 4194320 | tf_op jit(solution)/shard_map/all_gather | solution.py:94
  506.9 5.5 fusion.36
  513.3 139.6 %all-reduce.5.cloned.1.call-done = bf16[512,256]{1,0:T(8,128)(2,1)} async-done(((bf16[512,256]{1,0:T(8,128)(2,1)}), bf16[512,256]{1,0:T(8,128)(2,1)}) %all-reduce.5.cloned.1.call-update) | async-done | bytes 262160 | tf_op jit(solution)/shard_map/psum | solution.py:93
  653.0 2.0 convolution_multiply_fusion
  655.2 11.7 %cholesky.49 = f32[128,128]{1,0:T(8,128)S(1)} custom-call(f32[128,128]{1,0:T(8,128)S(1)} %cholesky.115), custom_call_target="Cholesky" | custom-call | tf_op jit(solution)/shard_map/jit(cholesky)/cholesky | solution.py:100
  667.0 9.8 %custom-call.15 = f32[1,128,128]{1,2,0:T(8,128)S(1)} custom-call(f32[1,128,128]{2,1,0:T(8,128)S(1)} %get-tuple-element.42), custom_call_target="InvertDiagBlocksLowerTriangular" | custom-call | tf_op jit(solution)/shard_map/jit(cholesky)/cholesky | solution.py:100
  677.3 11.7 %cholesky.103 = f32[128,128]{1,0:T(8,128)S(1)} custom-call(f32[128,128]{1,0:T(8,128)S(1)} %convolution_subtract_fusion.1), custom_call_target="Cholesky" | custom-call | tf_op jit(solution)/shard_map/jit(cholesky)/cholesky | solution.py:100
  691.1 4.2 while.1
  691.9 1.4 bitcast_dynamic-update-slice_fusion.2
  693.9 1.4 bitcast_dynamic-update-slice_fusion.2
  695.3 19.7 %custom-call.16 = f32[2,128,128]{1,2,0:T(8,128)S(1)} custom-call(f32[2,128,128]{2,1,0:T(8,128)S(1)} %get-tuple-element.10), custom_call_target="InvertDiagBlocksLowerTriangular" | custom-call | tf_op jit(solution)/shard_map/jit(_solve_triangular)/triangular_solve | solution.py:102
  716.7 4.3 fusion.23
  722.7 39.3 %reduce-scatter.5.cloned.1.call-done = bf16[64,256]{1,0:T(8,128)(2,1)} async-done(((bf16[512,256]{1,0:T(8,128)(2,1)}), bf16[64,256]{1,0:T(8,128)(2,1)}) %reduce-scatter.5.cloned.1.call-update) | async-done | bytes 32784 | tf_op jit(solution)/shard_map/reduce_scatter | solution.py:107
  762.0 1.4 bitcast_convert_fusion
  (76 shorter events, 14.8 us)
Async XLA Ops:
  7.2 372.4 %copy-start = (bf16[1,256,512]{2,1,0:T(8,128)(2,1)S(1)}, bf16[1,256,512]{2,1,0:T(8,128)(2,1)}, u32[]{:S(2)}) copy-start(bf16[1,256,512]{2,1,0:T(8,128)(2,1)} %param.10) | copy-start | bytes 786436
  7.2 372.4 %reduce-scatter.3.cloned.1.call-start = ((), (), s32[]{:S(2)}) async-start(), calls=%async_computation.2 | async-start | bytes 589824 | tf_op jit(solution)/shard_map/reduce_scatter | solution.py:78
  10.3 9.5 %collective-permute-start = (bf16[512,1,256]{0,2,1:T(8,128)(2,1)S(1)}, bf16[512,1,256]{0,2,1:T(8,128)(2,1)S(1)}, u32[]{:S(2)}, u32[]{:S(2)}) collective-permute-start(bf16[512,1,256]{0,2,1:T(8,128)(2,1)S(1)} %get-tuple-element.35), channel_id=1, source_target_pairs={{0,1},{1,2},{2,3},{3,4},{4,5},{5,6},{6,7},{8,9},{9,10},{10,11},{11... | collective-permute-start | bytes 786440 | tf_op jit(solution)/shard_map/ppermute | solution.py:18
  14.3 9.8 %collective-permute-start.1 = (bf16[512,1,256]{0,2,1:T(8,128)(2,1)S(1)}, bf16[512,1,256]{0,2,1:T(8,128)(2,1)S(1)}, u32[]{:S(2)}, u32[]{:S(2)}) collective-permute-start(bf16[512,1,256]{0,2,1:T(8,128)(2,1)S(1)} %get-tuple-element.36), channel_id=1, source_target_pairs={{1,0},{2,1},{3,2},{4,3},{5,4},{6,5},{7,6},{9,8},{10,9},{11,10},{12... | collective-permute-start | bytes 786440 | tf_op jit(solution)/shard_map/ppermute | solution.py:19
  30.3 14.7 %copy-start.4 = (bf16[1,256,256]{2,1,0:T(8,128)(2,1)S(1)}, bf16[1,256,256]{2,1,0:T(8,128)(2,1)}, u32[]{:S(2)}) copy-start(bf16[1,256,256]{2,1,0:T(8,128)(2,1)} %param.8) | copy-start | bytes 393220
  82.2 9.6 %copy-start.5 = (s32[1,512,2,4]{1,3,2,0:T(4,128)S(1)}, s32[1,512,2,4]{1,3,2,0:T(4,128)}, u32[]{:S(2)}) copy-start(s32[1,512,2,4]{1,3,2,0:T(4,128)} %param.12) | copy-start | bytes 49156
  86.8 47.7 %collective-permute-start.2 = (bf16[512,1,2048]{0,2,1:T(8,128)(2,1)}, bf16[512,1,2048]{0,2,1:T(8,128)(2,1)S(1)}, u32[]{:S(2)}, u32[]{:S(2)}) collective-permute-start(bf16[512,1,2048]{0,2,1:T(8,128)(2,1)} %get-tuple-element.27), channel_id=1, source_target_pairs={{0,1},{1,2},{2,3},{3,4},{4,5},{5,6},{6,7},{8,9},{9,10},{10,11},{11... | collective-permute-start | bytes 6291464 | tf_op jit(solution)/shard_map/ppermute | solution.py:18
  90.5 48.2 %collective-permute-start.3 = (bf16[512,1,2048]{0,2,1:T(8,128)(2,1)}, bf16[512,1,2048]{0,2,1:T(8,128)(2,1)}, u32[]{:S(2)}, u32[]{:S(2)}) collective-permute-start(bf16[512,1,2048]{0,2,1:T(8,128)(2,1)} %get-tuple-element.28), channel_id=1, source_target_pairs={{1,0},{2,1},{3,2},{4,3},{5,4},{6,5},{7,6},{9,8},{10,9},{11,10},{12... | collective-permute-start | bytes 6291464 | tf_op jit(solution)/shard_map/ppermute | solution.py:19
  299.3 13.1 %copy-start.1 = (bf16[1,4096,256]{2,1,0:T(8,128)(2,1)S(1)}, bf16[1,4096,256]{2,1,0:T(8,128)(2,1)}, u32[]{:S(2)}) copy-start(bf16[1,4096,256]{2,1,0:T(8,128)(2,1)} %param.9) | copy-start | bytes 6291460
  312.4 12.0 %slice-start = ((s8[8388608]{0:T(1024)(128)(4,1)}), s8[4194304]{0:T(1024)(128)(4,1)S(1)}, s32[]{:S(2)}) async-start(s8[8388608]{0:T(1024)(128)(4,1)} %bitcast.100), calls=%async_computation.7 | async-start | bytes 8388608
  318.4 6.0 slice-start.1
  329.0 8.6 %copy-start.6 = (s32[512]{0:T(512)S(1)}, s32[512]{0:T(512)}, u32[]{:S(2)}) copy-start(s32[512]{0:T(512)} %param.13) | copy-start | bytes 6148
  329.0 92.0 %copy-start.3 = (bf16[1,512,256]{2,1,0:T(8,128)(2,1)S(1)}, bf16[1,512,256]{2,1,0:T(8,128)(2,1)}, u32[]{:S(2)}) copy-start(bf16[1,512,256]{2,1,0:T(8,128)(2,1)} %param.11) | copy-start | bytes 786436
  337.5 81.8 %all-gather.5.cloned.1.call-start = ((), (), s32[]{:S(2)}) async-start(), calls=%async_computation.5 | async-start | bytes 1179648 | tf_op jit(solution)/shard_map/all_gather | solution.py:88
  381.5 125.4 %all-gather.7.cloned.1.call-start = ((), (), s32[]{:S(2)}) async-start(), calls=%async_computation.6 | async-start | bytes 4456448 | tf_op jit(solution)/shard_map/all_gather | solution.py:94
  512.4 140.6 %all-reduce.5.cloned.1.call-start = ((), (), s32[]{:S(2)}) async-start(), calls=%async_computation.3 | async-start | bytes 524288 | tf_op jit(solution)/shard_map/psum | solution.py:93
  512.9 249.1 %reduce-scatter.5.cloned.1.call-start = ((), (), s32[]{:S(2)}) async-start(), calls=%async_computation.4 | async-start | bytes 294912 | tf_op jit(solution)/shard_map/reduce_scatter | solution.py:107
  716.6 46.8 %copy-start.2 = (f32[64,256]{1,0:T(8,128)}, f32[64,256]{1,0:T(8,128)S(1)}, u32[]{:S(2)}) copy-start(f32[64,256]{1,0:T(8,128)S(1)} %maximum_bitcast_fusion) | copy-start | bytes 196612
Sparse Core Ops, SparseCore 0:
  337.6 41.8 reduce-scatter.2
  381.6 37.6 all-gather.4
  452.1 54.7 all-gather.6
  515.3 137.6 all-reduce.4
  722.8 39.1 reduce-scatter.4
